TPU v7x, 256 devices: a whole 4x4x8 slice. The times are simulated.
256 devices in a mesh: dp: 32 (over z, y), chan: 8 (over x, core).
Axes of the slice: x: 4, y: 4, z: 8, core: 2. Of those that a mesh axis runs over, the one named last changes fastest.
Arguments:
- inputs: bfloat16 [12544, 2048], P('dp', 'chan'), may hold values from -6 to 6
- conv_one: bfloat16 [9, 32, 2048], P(None, None, 'chan'), may hold values from -0.375 to 0.375
- conv_two: bfloat16 [9, 32, 2048], P(None, None, 'chan'), may hold values from -0.375 to 0.375
- probe_one: bfloat16 [2048, 512], P('chan'), may hold values from -0.125 to 0.125
- probe_two: bfloat16 [2048, 512], P('chan'), may hold values from -0.125 to 0.125
Outputs:
- restored: bfloat16 [12544, 2048], P('dp', 'chan')
- triangle: float32 [512, 512], replicated
All inputs are finite; a program needn't handle non-finite values.
Results may differ from a plain program's by a relative error of at most 0.028.
Values may be sent and summed in bfloat16 or wider, within the bound.
No kernel may reach another device: no remote copies, remote signals or barrier semaphores. Data moves between devices by JAX's collectives and lax.ppermute only.
A program may use at most 64 MiB of HBM per device.

v0:
```python
import math
import jax
import jax.numpy as jnp
from jax import lax
from jax.sharding import PartitionSpec as P

SIDE = 7


def convolve(field, weight):
    pixels, width = field.shape
    group_width = weight.shape[1]
    groups = width // group_width
    images = field.reshape(pixels // (SIDE * SIDE), SIDE, SIDE, width)
    padded = jnp.pad(images, ((0, 0), (1, 1), (1, 1), (0, 0)))
    total = jnp.zeros((pixels, groups, group_width), jnp.float32)
    for offset in range(9):
        row_shift = offset // 3
        col_shift = offset % 3
        window = padded[:, row_shift : row_shift + SIDE, col_shift : col_shift + SIDE, :]
        window = window.reshape(pixels, groups, group_width)
        kernel = weight[offset].reshape(group_width, groups, group_width)
        total = total + jnp.einsum(
            "pgi,igo->pgo", window, kernel, preferred_element_type=jnp.float32
        )
    return total.reshape(pixels, width).astype(jnp.bfloat16)


def gram_of(sketch):
    return lax.dot_general(
        sketch, sketch, (((0,), (0,)), ((), ())), preferred_element_type=jnp.float32
    )


def cross_of(sketch, responses):
    return lax.dot_general(
        sketch, responses, (((0,), (0,)), ((), ())), preferred_element_type=jnp.float32
    )


def finish(sketch, gram, cross):
    lower = jnp.linalg.cholesky(gram)
    coeffs = lax.linalg.triangular_solve(lower, cross, left_side=True, lower=True).astype(
        jnp.bfloat16
    )
    mapped = lax.linalg.triangular_solve(
        lower, coeffs.astype(jnp.float32), left_side=True, lower=True, transpose_a=True
    ).astype(jnp.bfloat16)
    return (jnp.dot(sketch, mapped, preferred_element_type=jnp.float32).astype(jnp.bfloat16), lower)


def compress(responses, probe):
    partial_sketch = jnp.dot(responses, probe, preferred_element_type=jnp.float32)
    sketch = lax.psum(partial_sketch, "chan").astype(jnp.bfloat16)
    gram, cross = lax.psum((gram_of(sketch), cross_of(sketch, responses)), "dp")
    return finish(sketch, gram, cross)


def per_device(inputs, conv_one, conv_two, probe_one, probe_two):
    responses_one = convolve(inputs, conv_one)
    restored_one, lower_one = compress(responses_one, probe_one)
    activated = jnp.maximum(restored_one, jnp.zeros((), jnp.bfloat16))
    responses_two = convolve(activated, conv_two)
    restored, lower_two = compress(responses_two, probe_two)
    total_rows = inputs.shape[0] * lax.axis_size("dp")
    triangle = jnp.transpose(lower_two) * (1.0 / math.sqrt(total_rows))
    return (restored, triangle)


def solution(mesh):
    in_specs = (
        P("dp", "chan"),
        P(None, None, "chan"),
        P(None, None, "chan"),
        P("chan", None),
        P("chan", None),
    )
    out_specs = (P("dp", "chan"), P())
    return jax.shard_map(
        per_device, mesh=mesh, in_specs=in_specs, out_specs=out_specs, check_vma=False
    )
```

profile of v0, /device:TPU:2, one launch (start us, length us, event | category | flops | bytes accessed | tf_op | source)
XLA Modules:
  0.0 705.7 jit_solution(17671794830554544109)
XLA Ops:
  31.8 28.5 %all-reduce.13 = bf16[392,512]{1,0:T(8,128)(2,1)S(1)} all-reduce(f32[392,512]{1,0:T(8,128)S(1)} %fusion.143), channel_id=1, replica_groups=mesh['dp'=32,'chan'=8] {'chan'}, use_global_device_ids=true, to_apply=%region_0.1 | all-reduce | flops 200704 | bytes 1204224 | tf_op jit(solution)/shard_map/psum | solution.py:54
  61.4 1.4 fusion.149
  69.7 149.1 %all-reduce.12.cloned.1.call-done = (f32[512,256]{1,0:T(8,128)}, f32[512,512]{0,1:T(8,128)}) async-done(((f32[512,256]{1,0:T(8,128)}, f32[512,512]{0,1:T(8,128)}), (f32[512,256]{1,0:T(8,128)}, f32[512,512]{0,1:T(8,128)})) %all-reduce.12.cloned.1.call-update) | async-done | bytes 1572880 | tf_op jit(solution)/shard_map/psum | solution.py:55
  218.8 1.6 copy.60
  221.6 11.7 %cholesky.286 = f32[128,128]{1,0:T(8,128)S(1)} custom-call(f32[128,128]{1,0:T(8,128)S(1)} %cholesky.426), custom_call_target="Cholesky" | custom-call | tf_op jit(solution)/shard_map/jit(cholesky)/cholesky | solution.py:42
  233.5 9.8 %custom-call.31 = f32[1,128,128]{1,2,0:T(8,128)S(1)} custom-call(f32[1,128,128]{2,1,0:T(8,128)S(1)} %get-tuple-element.120), custom_call_target="InvertDiagBlocksLowerTriangular" | custom-call | tf_op jit(solution)/shard_map/jit(cholesky)/cholesky | solution.py:42
  244.0 11.7 %cholesky.305 = f32[128,128]{1,0:T(8,128)S(1)} custom-call(f32[128,128]{1,0:T(8,128)S(1)} %cholesky.430), custom_call_target="Cholesky" | custom-call | tf_op jit(solution)/shard_map/jit(cholesky)/cholesky | solution.py:42
  255.8 10.2 %custom-call.32 = f32[1,128,128]{1,2,0:T(8,128)S(1)} custom-call(f32[1,128,128]{2,1,0:T(8,128)S(1)} %get-tuple-element.117), custom_call_target="InvertDiagBlocksLowerTriangular" | custom-call | tf_op jit(solution)/shard_map/jit(cholesky)/cholesky | solution.py:42
  266.6 11.7 %cholesky.326 = f32[128,128]{1,0:T(8,128)S(1)} custom-call(f32[128,128]{1,0:T(8,128)S(1)} %cholesky.435), custom_call_target="Cholesky" | custom-call | tf_op jit(solution)/shard_map/jit(cholesky)/cholesky | solution.py:42
  279.1 9.8 %custom-call.33 = f32[1,128,128]{1,2,0:T(8,128)S(1)} custom-call(f32[1,128,128]{2,1,0:T(8,128)S(1)} %get-tuple-element.114), custom_call_target="InvertDiagBlocksLowerTriangular" | custom-call | tf_op jit(solution)/shard_map/jit(cholesky)/cholesky | solution.py:42
  289.5 11.9 %cholesky.343 = f32[128,128]{1,0:T(8,128)S(1)} custom-call(f32[128,128]{1,0:T(8,128)S(1)} %convolution_subtract_fusion.17), custom_call_target="Cholesky" | custom-call | tf_op jit(solution)/shard_map/jit(cholesky)/cholesky | solution.py:42
  305.5 8.4 %while.8 = (s32[]{:T(128)}, f32[512,512]{1,0:T(8,128)S(1)}, s32[4,2]{0,1:T(2,128)S(1)}, f32[4,128,128]{2,1,0:T(8,128)S(1)}, s32[]{:T(128)}) while((s32[]{:T(128)}, f32[512,512]{1,0:T(8,128)S(1)}, s32[4,2]{0,1:T(2,128)S(1)}, f32[4,128,128]{2,1,0:T(8,128)S(1)}, s32[]{:T(128)}) %tuple.96), condition=%wide.while_cond.1, body=%wide.while_body.1.sunk | while | flops 2 | bytes 131181 | solution.py:46
  306.1 1.4 bitcast_dynamic-update-slice_fusion.4
  308.2 1.4 bitcast_dynamic-update-slice_fusion.4
  313.8 39.3 %custom-call.35 = f32[4,128,128]{1,2,0:T(8,128)S(1)} custom-call(f32[4,128,128]{2,1,0:T(8,128)S(1)} %get-tuple-element.34), custom_call_target="InvertDiagBlocksLowerTriangular" | custom-call | tf_op jit(solution)/shard_map/triangular_solve/custom-call.8 | solution.py:46
  376.4 26.7 %all-reduce.14 = bf16[392,512]{1,0:T(8,128)(2,1)S(1)} all-reduce(f32[392,512]{1,0:T(8,128)S(1)} %fusion.145), channel_id=1, replica_groups=mesh['dp'=32,'chan'=8] {'chan'}, use_global_device_ids=true, to_apply=%region_11.15 | all-reduce | flops 200704 | bytes 1204224 | tf_op jit(solution)/shard_map/psum | solution.py:54
  403.1 1.5 fusion.147
  405.7 150.2 %all-reduce.10.cloned.1.call-done = (f32[512,256]{1,0:T(8,128)}, f32[512,512]{0,1:T(8,128)}) async-done(((f32[512,256]{1,0:T(8,128)}, f32[512,512]{0,1:T(8,128)}), (f32[512,256]{1,0:T(8,128)}, f32[512,512]{0,1:T(8,128)})) %all-reduce.10.cloned.1.call-update) | async-done | bytes 1572880 | tf_op jit(solution)/shard_map/psum | solution.py:55
  555.9 1.6 copy.80
  558.8 11.7 %cholesky.358 = f32[128,128]{1,0:T(8,128)S(1)} custom-call(f32[128,128]{1,0:T(8,128)S(1)} %cholesky.439), custom_call_target="Cholesky" | custom-call | tf_op jit(solution)/shard_map/jit(cholesky)/cholesky | solution.py:42
  570.6 9.8 %custom-call.36 = f32[1,128,128]{1,2,0:T(8,128)S(1)} custom-call(f32[1,128,128]{2,1,0:T(8,128)S(1)} %get-tuple-element.110), custom_call_target="InvertDiagBlocksLowerTriangular" | custom-call | tf_op jit(solution)/shard_map/jit(cholesky)/cholesky | solution.py:42
  581.1 11.7 %cholesky.377 = f32[128,128]{1,0:T(8,128)S(1)} custom-call(f32[128,128]{1,0:T(8,128)S(1)} %cholesky.443), custom_call_target="Cholesky" | custom-call | tf_op jit(solution)/shard_map/jit(cholesky)/cholesky | solution.py:42
  594.2 9.9 %custom-call.37 = f32[1,128,128]{1,2,0:T(8,128)S(1)} custom-call(f32[1,128,128]{2,1,0:T(8,128)S(1)} %get-tuple-element.107), custom_call_target="InvertDiagBlocksLowerTriangular" | custom-call | tf_op jit(solution)/shard_map/jit(cholesky)/cholesky | solution.py:42
  604.8 11.7 %cholesky.398 = f32[128,128]{1,0:T(8,128)S(1)} custom-call(f32[128,128]{1,0:T(8,128)S(1)} %cholesky.448), custom_call_target="Cholesky" | custom-call | tf_op jit(solution)/shard_map/jit(cholesky)/cholesky | solution.py:42
  617.2 9.8 %custom-call.38 = f32[1,128,128]{1,2,0:T(8,128)S(1)} custom-call(f32[1,128,128]{2,1,0:T(8,128)S(1)} %get-tuple-element.104), custom_call_target="InvertDiagBlocksLowerTriangular" | custom-call | tf_op jit(solution)/shard_map/jit(cholesky)/cholesky | solution.py:42
  627.6 11.9 %cholesky.415 = f32[128,128]{1,0:T(8,128)S(1)} custom-call(f32[128,128]{1,0:T(8,128)S(1)} %convolution_subtract_fusion.16), custom_call_target="Cholesky" | custom-call | tf_op jit(solution)/shard_map/jit(cholesky)/cholesky | solution.py:42
  644.0 8.4 %while.9 = (s32[]{:T(128)}, f32[512,512]{1,0:T(8,128)S(1)}, s32[4,2]{0,1:T(2,128)S(1)}, f32[4,128,128]{2,1,0:T(8,128)S(1)}, s32[]{:T(128)}) while((s32[]{:T(128)}, f32[512,512]{1,0:T(8,128)S(1)}, s32[4,2]{0,1:T(2,128)S(1)}, f32[4,128,128]{2,1,0:T(8,128)S(1)}, s32[]{:T(128)}) %tuple.108), condition=%wide.while_cond.1.clone, body=%wide.while_body.1.clone.sunk | while | flops 2 | bytes 131181 | solution.py:46
  644.7 1.4 bitcast_dynamic-update-slice_fusion.5
  646.8 1.4 bitcast_dynamic-update-slice_fusion.5
  648.9 1.4 bitcast_dynamic-update-slice_fusion.5
  651.0 1.4 bitcast_dynamic-update-slice_fusion.5
  652.4 39.3 %custom-call.40 = f32[4,128,128]{1,2,0:T(8,128)S(1)} custom-call(f32[4,128,128]{2,1,0:T(8,128)S(1)} %get-tuple-element.36), custom_call_target="InvertDiagBlocksLowerTriangular" | custom-call | tf_op jit(solution)/shard_map/triangular_solve/custom-call.8 | solution.py:46
  (238 shorter events, 84.1 us)
Async XLA Ops:
  7.2 24.3 %copy-start = (bf16[256,512]{1,0:T(8,128)(2,1)S(1)}, bf16[256,512]{1,0:T(8,128)(2,1)}, u32[]{:S(2)}) copy-start(bf16[256,512]{1,0:T(8,128)(2,1)} %param.13) | copy-start | bytes 786436
  7.2 1.1 copy-start.18
  7.2 211.6 %all-reduce.12.cloned.1.call-start = ((), (), s32[]{:S(2)}) async-start(), calls=%async_computation.1 | async-start | bytes 3145728 | tf_op jit(solution)/shard_map/psum | solution.py:55
  8.3 0.9 copy-start.36
  23.5 1.3 copy-start.22
  25.3 1.2 copy-start.4
  26.1 1.2 copy-start.5
  27.5 0.9 copy-start.16
  27.5 1.0 copy-start.28
  27.5 1.3 copy-start.6
  29.4 1.1 copy-start.7
  29.4 1.1 copy-start.35
  62.8 493.0 %all-reduce.10.cloned.1.call-start = ((), (), s32[]{:S(2)}) async-start(), calls=%async_computation | async-start | bytes 3145728 | tf_op jit(solution)/shard_map/psum | solution.py:55
  218.8 1.7 copy-start.1
  220.6 1.0 copy-start.14
  221.6 21.7 %copy-start.15 = (f32[512,512]{1,0:T(8,128)S(1)}, f32[512,512]{1,0:T(8,128)}, u32[]{:S(2)}) copy-start(f32[512,512]{1,0:T(8,128)} %copy-done.14) | copy-start | bytes 3145732
  305.3 47.9 %copy-start.19 = (f32[512,256]{1,0:T(8,128)S(1)}, f32[512,256]{1,0:T(8,128)}, u32[]{:S(2)}) copy-start(f32[512,256]{1,0:T(8,128)} %get-tuple-element.59) | copy-start | bytes 1572868
  367.3 1.4 copy-start.17
  367.3 1.4 copy-start.27
  367.3 1.6 copy-start.11
  369.6 1.1 copy-start.10
  369.6 1.1 copy-start.32
  371.5 1.1 copy-start.9
  371.5 1.1 copy-start.31
  372.7 1.1 copy-start.8
  372.7 1.1 copy-start.30
  375.1 1.0 copy-start.26
  555.9 1.7 copy-start.2
  557.8 1.0 copy-start.12
  558.8 21.7 %copy-start.13 = (f32[512,512]{1,0:T(8,128)S(1)}, f32[512,512]{1,0:T(8,128)}, u32[]{:S(2)}) copy-start(f32[512,512]{1,0:T(8,128)} %copy-done.12) | copy-start | bytes 3145732
  642.8 48.9 %copy-start.20 = (f32[512,256]{1,0:T(8,128)S(1)}, f32[512,256]{1,0:T(8,128)}, u32[]{:S(2)}) copy-start(f32[512,256]{1,0:T(8,128)} %get-tuple-element.57) | copy-start | bytes 1572868
  696.1 1.2 copy-start.3
  (8 other events, 7.0 us)
Sparse Core Ops, SparseCore 0:
  63.0 155.7 all-reduce.11
  405.8 149.9 all-reduce.9
where the time goes:
time: 713 us; the launch traced here: 706 us
  waiting for transfers between devices  299 us (42%)
  other arithmetic  239 us (34%)
  local copies, waits for them, and re-layouts  62.7 us (9%)
  blocking collectives  55.2 us (8%)
  matrix products  29 us (4%)
  between operations  20.4 us (3%)
    psum x2, waiting for transfers between devices, compress(): gram, cross = lax.psum((gram_of(sketch), cross_of(sketch, responses)), 'dp')  299 us
    another operation x29, other arithmetic, finish(): lower = jnp.linalg.cholesky(gram)  158 us
    another operation x4, other arithmetic, finish(): lax.linalg.triangular_solve(lower, coeffs.astype(jnp.float32), left_side=...  78.8 us
    psum x2, blocking collectives, compress(): sketch = lax.psum(partial_sketch, 'chan').astype(jnp.bfloat16)  55.2 us
    another operation x27, local copies, waits for them, and re-layouts, finish(): lax.linalg.triangular_solve(lower, coeffs.astype(jnp.float32), left_side=...  16.6 us
    reshape x16, local copies, waits for them, and re-layouts, convolve(): window = window.reshape(pixels, groups, group_width)  14.8 us
  transfers between devices with their start and end apart: 2, of which 2 were waited for; matrix products, arithmetic and copies ran while one was open for 1% of the time, Pallas kernels for 0%

commit v1 on v0

--- a/solution.py
+++ b/solution.py
@@ -51,7 +51,7 @@
 
 def compress(responses, probe):
     partial_sketch = jnp.dot(responses, probe, preferred_element_type=jnp.float32)
-    sketch = lax.psum(partial_sketch, "chan").astype(jnp.bfloat16)
+    sketch = jnp.sum(lax.all_gather(partial_sketch, "chan"), axis=0).astype(jnp.bfloat16)
     gram, cross = lax.psum((gram_of(sketch), cross_of(sketch, responses)), "dp")
     return finish(sketch, gram, cross)
 

time: 713 us -> 761 us (1.067)
  waiting for transfers between devices: 299 us -> 386 us
  blocking collectives: 55.2 us -> 0 us
  matrix products: 29 us -> 42.6 us
  other arithmetic: 239 us -> 249 us
    all_gather x0 -> x2, waiting for transfers between devices: none -> 86.2 us  [compress(): lax.all_gather(partial_sketch, 'chan')]
    psum x2 -> x0, blocking collectives: 55.2 us -> none  [compress(): sketch = lax.psum(partial_sketch, 'chan').astype(jnp.bfloat16)]
    dot_general x18, matrix products: 9.41 us -> 17.6 us  [convolve(): jnp.einsum('pgi,igo->pgo', window, kernel, preferred_element_type=jnp.flo...]
  transfers between devices with their start and end apart: 2 -> 4, of which waited for: 2 -> 4; matrix products, arithmetic and copies ran while one was open for 1% -> 1% of each run, Pallas kernels for 0% -> 0%
where the time goes in v1:
time: 761 us; the launch traced here: 754 us
  waiting for transfers between devices  386 us (51%)
  other arithmetic  249 us (33%)
  local copies, waits for them, and re-layouts  55.3 us (7%)
  matrix products  42.6 us (6%)
  between operations  20 us (3%)
    psum x2, waiting for transfers between devices, compress(): gram, cross = lax.psum((gram_of(sketch), cross_of(sketch, responses)), 'dp')  299 us
    another operation x29, other arithmetic, finish(): lower = jnp.linalg.cholesky(gram)  158 us
    all_gather x2, waiting for transfers between devices, compress(): lax.all_gather(partial_sketch, 'chan')  86.2 us
    another operation x4, other arithmetic, finish(): lax.linalg.triangular_solve(lower, coeffs.astype(jnp.float32), left_side=...  79.6 us
    dot_general x18, matrix products, convolve(): jnp.einsum('pgi,igo->pgo', window, kernel, preferred_element_type=jnp.flo...  17.6 us
    another operation x27, local copies, waits for them, and re-layouts, finish(): lax.linalg.triangular_solve(lower, coeffs.astype(jnp.float32), left_side=...  16.3 us
  transfers between devices with their start and end apart: 4, of which 4 were waited for; matrix products, arithmetic and copies ran while one was open for 1% of the time, Pallas kernels for 0%

profile of v1, /device:TPU:2, one launch (start us, length us, event | category | flops | bytes accessed | tf_op | source)
XLA Modules:
  0.0 753.9 jit_solution(16377027552630394740)
XLA Ops:
  8.3 1.8 copy.50
  29.3 1.6 convolution_bitcast_fusion.3
  30.9 1.6 convolution_bitcast_fusion.4
  35.4 46.2 %all-gather.5.cloned.1.call-done = f32[3136,512]{1,0:T(8,128)} async-done(((f32[392,512]{1,0:T(8,128)}), f32[3136,512]{1,0:T(8,128)}) %all-gather.5.cloned.1.call-update) | async-done | bytes 6422544 | tf_op jit(solution)/shard_map/all_gather | solution.py:54
  81.6 3.6 reduce_sum.18
  94.1 146.6 %all-reduce.10.cloned.1.call-done = (f32[512,256]{1,0:T(8,128)}, f32[512,512]{0,1:T(8,128)}) async-done(((f32[512,256]{1,0:T(8,128)}, f32[512,512]{0,1:T(8,128)}), (f32[512,256]{1,0:T(8,128)}, f32[512,512]{0,1:T(8,128)})) %all-reduce.10.cloned.1.call-update) | async-done | bytes 1572880 | tf_op jit(solution)/shard_map/psum | solution.py:55
  240.7 1.6 copy.60
  244.8 11.7 %cholesky.286 = f32[128,128]{1,0:T(8,128)S(1)} custom-call(f32[128,128]{1,0:T(8,128)S(1)} %cholesky.426), custom_call_target="Cholesky" | custom-call | tf_op jit(solution)/shard_map/jit(cholesky)/cholesky | solution.py:42
  256.6 9.8 %custom-call.31 = f32[1,128,128]{1,2,0:T(8,128)S(1)} custom-call(f32[1,128,128]{2,1,0:T(8,128)S(1)} %get-tuple-element.120), custom_call_target="InvertDiagBlocksLowerTriangular" | custom-call | tf_op jit(solution)/shard_map/jit(cholesky)/cholesky | solution.py:42
  269.0 11.7 %cholesky.305 = f32[128,128]{1,0:T(8,128)S(1)} custom-call(f32[128,128]{1,0:T(8,128)S(1)} %cholesky.430), custom_call_target="Cholesky" | custom-call | tf_op jit(solution)/shard_map/jit(cholesky)/cholesky | solution.py:42
  280.7 10.2 %custom-call.32 = f32[1,128,128]{1,2,0:T(8,128)S(1)} custom-call(f32[1,128,128]{2,1,0:T(8,128)S(1)} %get-tuple-element.117), custom_call_target="InvertDiagBlocksLowerTriangular" | custom-call | tf_op jit(solution)/shard_map/jit(cholesky)/cholesky | solution.py:42
  292.5 11.7 %cholesky.326 = f32[128,128]{1,0:T(8,128)S(1)} custom-call(f32[128,128]{1,0:T(8,128)S(1)} %cholesky.435), custom_call_target="Cholesky" | custom-call | tf_op jit(solution)/shard_map/jit(cholesky)/cholesky | solution.py:42
  304.9 9.8 %custom-call.33 = f32[1,128,128]{1,2,0:T(8,128)S(1)} custom-call(f32[1,128,128]{2,1,0:T(8,128)S(1)} %get-tuple-element.114), custom_call_target="InvertDiagBlocksLowerTriangular" | custom-call | tf_op jit(solution)/shard_map/jit(cholesky)/cholesky | solution.py:42
  316.2 11.9 %cholesky.343 = f32[128,128]{1,0:T(8,128)S(1)} custom-call(f32[128,128]{1,0:T(8,128)S(1)} %convolution_subtract_fusion.17), custom_call_target="Cholesky" | custom-call | tf_op jit(solution)/shard_map/jit(cholesky)/cholesky | solution.py:42
  332.1 7.9 %while.8 = (s32[]{:T(128)}, f32[512,512]{1,0:T(8,128)S(1)}, s32[4,2]{0,1:T(2,128)S(1)}, f32[4,128,128]{2,1,0:T(8,128)S(1)}, s32[]{:T(128)}) while((s32[]{:T(128)}, f32[512,512]{1,0:T(8,128)S(1)}, s32[4,2]{0,1:T(2,128)S(1)}, f32[4,128,128]{2,1,0:T(8,128)S(1)}, s32[]{:T(128)}) %tuple.96), condition=%wide.while_cond.1, body=%wide.while_body.1.sunk | while | flops 2 | bytes 131181 | solution.py:46
  340.1 39.3 %custom-call.35 = f32[4,128,128]{1,2,0:T(8,128)S(1)} custom-call(f32[4,128,128]{2,1,0:T(8,128)S(1)} %get-tuple-element.34), custom_call_target="InvertDiagBlocksLowerTriangular" | custom-call | tf_op jit(solution)/shard_map/triangular_solve/custom-call.8 | solution.py:46
  395.4 1.6 convolution_add_fusion.6
  397.0 1.6 convolution_add_fusion.5
  403.5 40.0 %all-gather.7.cloned.1.call-done = f32[3136,512]{1,0:T(8,128)} async-done(((f32[392,512]{1,0:T(8,128)}), f32[3136,512]{1,0:T(8,128)}) %all-gather.7.cloned.1.call-update) | async-done | bytes 6422544 | tf_op jit(solution)/shard_map/all_gather | solution.py:54
  443.5 3.6 reduce_sum.19
  449.8 152.9 %all-reduce.8.cloned.1.call-done = (f32[512,256]{1,0:T(8,128)}, f32[512,512]{0,1:T(8,128)}) async-done(((f32[512,256]{1,0:T(8,128)}, f32[512,512]{0,1:T(8,128)}), (f32[512,256]{1,0:T(8,128)}, f32[512,512]{0,1:T(8,128)})) %all-reduce.8.cloned.1.call-update) | async-done | bytes 1572880 | tf_op jit(solution)/shard_map/psum | solution.py:55
  602.6 1.6 copy.80
  604.2 1.5 fusion.10
  605.7 11.7 %cholesky.358 = f32[128,128]{1,0:T(8,128)S(1)} custom-call(f32[128,128]{1,0:T(8,128)S(1)} %cholesky.439), custom_call_target="Cholesky" | custom-call | tf_op jit(solution)/shard_map/jit(cholesky)/cholesky | solution.py:42
  617.6 9.8 %custom-call.36 = f32[1,128,128]{1,2,0:T(8,128)S(1)} custom-call(f32[1,128,128]{2,1,0:T(8,128)S(1)} %get-tuple-element.110), custom_call_target="InvertDiagBlocksLowerTriangular" | custom-call | tf_op jit(solution)/shard_map/jit(cholesky)/cholesky | solution.py:42
  628.1 11.9 %cholesky.377 = f32[128,128]{1,0:T(8,128)S(1)} custom-call(f32[128,128]{1,0:T(8,128)S(1)} %cholesky.443), custom_call_target="Cholesky" | custom-call | tf_op jit(solution)/shard_map/jit(cholesky)/cholesky | solution.py:42
  641.3 9.8 %custom-call.37 = f32[1,128,128]{1,2,0:T(8,128)S(1)} custom-call(f32[1,128,128]{2,1,0:T(8,128)S(1)} %get-tuple-element.107), custom_call_target="InvertDiagBlocksLowerTriangular" | custom-call | tf_op jit(solution)/shard_map/jit(cholesky)/cholesky | solution.py:42
  651.7 11.7 %cholesky.398 = f32[128,128]{1,0:T(8,128)S(1)} custom-call(f32[128,128]{1,0:T(8,128)S(1)} %cholesky.448), custom_call_target="Cholesky" | custom-call | tf_op jit(solution)/shard_map/jit(cholesky)/cholesky | solution.py:42
  664.2 9.8 %custom-call.38 = f32[1,128,128]{1,2,0:T(8,128)S(1)} custom-call(f32[1,128,128]{2,1,0:T(8,128)S(1)} %get-tuple-element.104), custom_call_target="InvertDiagBlocksLowerTriangular" | custom-call | tf_op jit(solution)/shard_map/jit(cholesky)/cholesky | solution.py:42
  674.6 11.9 %cholesky.415 = f32[128,128]{1,0:T(8,128)S(1)} custom-call(f32[128,128]{1,0:T(8,128)S(1)} %convolution_subtract_fusion.16), custom_call_target="Cholesky" | custom-call | tf_op jit(solution)/shard_map/jit(cholesky)/cholesky | solution.py:42
  690.9 8.5 %while.9 = (s32[]{:T(128)}, f32[512,512]{1,0:T(8,128)S(1)}, s32[4,2]{0,1:T(2,128)S(1)}, f32[4,128,128]{2,1,0:T(8,128)S(1)}, s32[]{:T(128)}) while((s32[]{:T(128)}, f32[512,512]{1,0:T(8,128)S(1)}, s32[4,2]{0,1:T(2,128)S(1)}, f32[4,128,128]{2,1,0:T(8,128)S(1)}, s32[]{:T(128)}) %tuple.112), condition=%wide.while_cond.1.clone, body=%wide.while_body.1.clone.sunk | while | flops 2 | bytes 131181 | solution.py:46
  700.1 40.1 %custom-call.40 = f32[4,128,128]{1,2,0:T(8,128)S(1)} custom-call(f32[4,128,128]{2,1,0:T(8,128)} %copy-done.11), custom_call_target="InvertDiagBlocksLowerTriangular" | custom-call | tf_op jit(solution)/shard_map/triangular_solve/custom-call.8 | solution.py:46
  (208 shorter events, 95.1 us)
Async XLA Ops:
  7.2 27.0 %copy-start = (bf16[256,512]{1,0:T(8,128)(2,1)S(1)}, bf16[256,512]{1,0:T(8,128)(2,1)}, u32[]{:S(2)}) copy-start(bf16[256,512]{1,0:T(8,128)(2,1)} %param.13) | copy-start | bytes 786436
  7.2 74.4 %all-gather.5.cloned.1.call-start = ((), (), s32[]{:S(2)}) async-start(), calls=%async_computation | async-start | bytes 7225344 | tf_op jit(solution)/shard_map/all_gather | solution.py:54
  25.2 7.2 copy-start.8
  25.3 7.2 copy-start.13
  25.3 7.4 copy-start.3
  25.3 7.4 copy-start.17
  25.3 7.9 %copy-start.4 = (bf16[392,8,32]{2,1,0:T(8,128)(2,1)S(1)}, bf16[392,8,32]{2,1,0:T(8,128)(2,1)}, u32[]{:S(2)}) copy-start(bf16[392,8,32]{2,1,0:T(8,128)(2,1)} %reshape.120) | copy-start | bytes 602116
  25.3 7.9 %copy-start.18 = (bf16[1,32,256]{1,2,0:T(8,128)(2,1)S(1)}, bf16[1,32,256]{1,2,0:T(8,128)(2,1)}, u32[]{:S(2)}) copy-start(bf16[1,32,256]{1,2,0:T(8,128)(2,1)} %copy.45) | copy-start | bytes 49156
  35.4 52.8 %copy-start.19 = (bf16[9,32,256]{2,1,0:T(8,128)(2,1)S(1)}, bf16[9,32,256]{2,1,0:T(8,128)(2,1)}, u32[]{:S(2)}) copy-start(bf16[9,32,256]{2,1,0:T(8,128)(2,1)} %param.12) | copy-start | bytes 442372
  35.4 205.3 %all-reduce.10.cloned.1.call-start = ((), (), s32[]{:S(2)}) async-start(), calls=%async_computation.3 | async-start | bytes 3145728 | tf_op jit(solution)/shard_map/psum | solution.py:55
  87.9 355.6 %all-gather.7.cloned.1.call-start = ((), (), s32[]{:S(2)}) async-start(), calls=%async_computation.1 | async-start | bytes 7225344 | tf_op jit(solution)/shard_map/all_gather | solution.py:54
  240.7 138.7 %copy-start.9 = (f32[512,256]{1,0:T(8,128)S(1)}, f32[512,256]{1,0:T(8,128)}, u32[]{:S(2)}) copy-start(f32[512,256]{1,0:T(8,128)} %get-tuple-element.59) | copy-start | bytes 1572868
  243.8 1.0 copy-start.7
  392.9 7.0 copy-start.6
  392.9 7.0 copy-start.16
  392.9 7.5 copy-start.5
  392.9 7.5 copy-start.15
  392.9 8.0 %copy-start.14 = (bf16[1,32,256]{1,2,0:T(8,128)(2,1)S(1)}, bf16[1,32,256]{1,2,0:T(8,128)(2,1)}, u32[]{:S(2)}) copy-start(bf16[1,32,256]{1,2,0:T(8,128)(2,1)} %copy.75) | copy-start | bytes 49156
  395.4 6.4 copy-start.12
  403.0 199.6 %all-reduce.8.cloned.1.call-start = ((), (), s32[]{:S(2)}) async-start(), calls=%async_computation.2 | async-start | bytes 3145728 | tf_op jit(solution)/shard_map/psum | solution.py:55
  604.2 136.0 %copy-start.10 = (f32[512,256]{1,0:T(8,128)S(1)}, f32[512,256]{1,0:T(8,128)}, u32[]{:S(2)}) copy-start(f32[512,256]{1,0:T(8,128)} %get-tuple-element.57) | copy-start | bytes 1572868
  689.8 57.3 %copy-start.1 = (bf16[256,512]{1,0:T(8,128)(2,1)S(1)}, bf16[256,512]{1,0:T(8,128)(2,1)}, u32[]{:S(2)}) copy-start(bf16[256,512]{1,0:T(8,128)(2,1)} %param.13) | copy-start | bytes 786436
  690.9 54.9 %copy-start.2 = (f32[512,512]{0,1:T(8,128)S(1)}, f32[512,512]{0,1:T(8,128)}, u32[]{:S(2)}) copy-start(f32[512,512]{0,1:T(8,128)} %get-tuple-element.65) | copy-start | bytes 3145732
  699.4 0.7 copy-start.11
Sparse Core Ops, SparseCore 0:
  35.5 46.0 all-gather.4
  88.0 152.6 all-reduce.9
  403.1 40.3 all-gather.6
  449.9 152.6 all-reduce.7
